TPU v7x, 32 devices: a whole 2x2x4 slice. The times are simulated.
32 devices in a mesh: vec: 8 (over z, core), rep: 4 (over y, x).
Axes of the slice: x: 2, y: 2, z: 4, core: 2. Of those that a mesh axis runs over, the one named last changes fastest.
Arguments:
- vectors: bfloat16 [1024, 1024], P('vec'), may hold values from 0 to 2
- pivot_index: int32 [4, 8], P('rep'), may hold values from 0 to 1023
Outputs:
- similarity: bfloat16 [7, 32, 1024, 128], P(None, 'rep', 'vec')
All inputs are finite; a program needn't handle non-finite values.
Results may differ from a plain program's by a relative error of at most 0.011.
Values may be sent and summed in bfloat16 or wider, within the bound.
A program may use at most 64 MiB of HBM per device.

v0:
```python
import functools
import math

import jax
import jax.numpy as jnp
from jax import lax
from jax.experimental import pallas as pl
from jax.experimental.pallas import tpu as pltpu
from jax.sharding import PartitionSpec as P

HALF = 3


def contract(left, right):
    return lax.dot_general(
        left, right, (((1,), (1,)), ((), ())), preferred_element_type=jnp.float32
    )


def arrival(chip, chips):
    first_chip = 1 - (chip + chips - 1) // chips
    last_chip = (chip + 1) // chips
    edge = first_chip + last_chip
    return first_chip, last_chip, edge, (first_chip, 1 + edge, 2 - 2 * edge + last_chip)


def places(s, core):
    is_far = s // 2
    own = HALF + (4 * s - 2) * (1 - is_far)
    other = HALF + (4 * s - 1 - 2 * core) * (1 - is_far) + (6 * core - 3) * is_far
    return is_far, own, other


def products(scaled, win, slot, count, block_rows):
    fields = scaled.shape[1]
    right = win[pl.ds(slot, 2)].reshape(2 * block_rows, fields)
    value = (contract(scaled[...], right) * (1.0 / math.sqrt(fields))).astype(jnp.bfloat16)
    shape = (count, block_rows, block_rows)
    return value[:, :block_rows].reshape(shape), value[:, block_rows:].reshape(shape)


def closing(n_vec, held, win, scaled, out_ref, last, sems):
    window, count, block_rows, _ = held.shape
    me = lax.axis_index("vec")
    core = me % 2
    s = arrival(me // 2, n_vec // 2)[3][2]
    is_far, own, other = places(s, core)
    own = own * (1 - is_far) + other * is_far

    def ready(i):
        return pltpu.make_async_copy(held.at[i], out_ref.at[i], sems.at[i])

    def late(i, place):
        return pltpu.make_async_copy(last.at[i], out_ref.at[place], sems.at[window + i])

    for i in range(window):
        pl.when(jnp.logical_and(own != i, other != i))(lambda i=i: ready(i).start())
    left, right = products(scaled, win, 2 + 2 * s, count, block_rows)
    last[0] = left
    last[1] = right
    pl.when(is_far == 0)(lambda: late(0, own).start())
    late(1, other).start()
    for i in range(window):
        pl.when(jnp.logical_and(own != i, other != i))(lambda i=i: ready(i).wait())
    pl.when(is_far == 0)(lambda: late(0, own).wait())
    late(1, other).wait()


def kernel(
    n_vec, n_a, n_b, vec_ref, index_ref, out_ref, win, scaled, wanted_ref, rows_ref, heard,
    z_send, z_recv, d_send, d_recv, r_send, r_recv, p_send, p_recv, c_send, c_recv, local_sem,
):
    block_rows, fields = vec_ref.shape
    count = index_ref.shape[1]
    n_rep = n_a * n_b
    chips = n_vec // 2
    part = block_rows // n_rep
    me = lax.axis_index("vec")
    rep = lax.axis_index("rep")
    a, b = rep // n_b, rep % n_b
    chip, core = me // 2, me % 2
    partner = me + 1 - 2 * core

    def at_vec(offset):
        return {"vec": (me + offset + n_vec) % n_vec}

    def rep_of(da, db):
        return ((a + da + n_a) % n_a) * n_b + (b + db + n_b) % n_b

    direct = [(0, i) for i in range(1, n_b)] + [(i, 0) for i in range(1, n_a)]
    diagonal = [(i, j) for i in range(1, n_a) for j in range(1, n_b)]
    short = n_vec <= 16

    own_copy = pltpu.make_async_copy(vec_ref, win.at[0], local_sem.at[0])
    index_copy = pltpu.make_async_copy(index_ref, wanted_ref, local_sem.at[1])
    own_copy.start()
    index_copy.start()

    barrier = pltpu.get_barrier_semaphore()

    def greet(i, carry):
        pl.semaphore_signal(barrier, inc=1, device_id=at_vec(2 * i))
        return carry

    lax.fori_loop(1, chips, greet, 0, unroll=short)
    pl.semaphore_signal(barrier, inc=1, device_id={"vec": partner})
    for da, db in direct:
        pl.semaphore_signal(barrier, inc=1, device_id={"rep": rep_of(da, db)})
    own_copy.wait()
    index_copy.wait()
    pl.semaphore_wait(barrier, chips + len(direct))

    def remote(src, dst, send_sem, recv_sem, device):
        return pltpu.make_async_remote_copy(
            src_ref=src, dst_ref=dst, send_sem=send_sem, recv_sem=recv_sem, device_id=device
        )

    started = []

    def start(copy):
        copy.start()
        started.append(copy)

    own_rows = pl.ds(pl.multiple_of(rep * part, part), part)
    far = 4 * (2 * core - 1)
    first_chip, last_chip, edge, order = arrival(chip, chips)
    outgoing = (last_chip, 1 + edge, 2 - 2 * edge + first_chip)

    def z_copy(s):
        is_far = s // 2
        offset = (2 - 4 * s) * (1 - is_far) + far * is_far
        return remote(
            win.at[0, own_rows], win.at[2 + 2 * s, own_rows], z_send.at[s], z_recv.at[s], at_vec(offset)
        )

    for s in outgoing:
        start(z_copy(s))
    partner_own = remote(win.at[0], win.at[1], c_send.at[0], c_recv.at[0], {"vec": partner})
    start(partner_own)

    wanted = wanted_ref[...] - me * block_rows
    spots = lax.broadcasted_iota(jnp.int32, (block_rows, count), 0)
    onehot = (spots == wanted).astype(jnp.bfloat16)
    mine = lax.dot_general(
        onehot, win[0], (((0,), (0,)), ((), ())), preferred_element_type=jnp.float32
    )
    rows_ref[...] = mine.astype(jnp.bfloat16)

    def rows_out(i):
        return remote(rows_ref, heard.at[i], p_send.at[i], p_recv.at[i], at_vec(2 * i))

    rows_partner = remote(rows_ref, heard.at[0], p_send.at[0], p_recv.at[0], {"vec": partner})

    def rows_across(i):
        k = chips - 1 + i
        return remote(heard.at[i], heard.at[k], p_send.at[k], p_recv.at[k], {"vec": partner})

    def loop(action):
        def body(i, carry):
            action(i)
            return carry

        lax.fori_loop(1, chips, body, 0, unroll=short)

    per_slot = 1 + len(direct) + 2 * len(diagonal)
    everything = pl.ds(0, fields)

    def rows_from(da, db):
        return pl.ds(pl.multiple_of(rep_of(-da, -db) * part, part), part)

    def half_from(da, db, h):
        start_row = rep_of(-da, -db) * part + h * (part // 2)
        return pl.ds(pl.multiple_of(start_row, part // 2), part // 2)

    def hand(s, number):
        if number == 0:
            rows, columns = own_rows, everything
        elif number <= len(direct):
            rows, columns = rows_from(*direct[number - 1]), everything
        else:
            which = number - 1 - len(direct)
            rows, columns = half_from(*diagonal[which // 2], which % 2), everything
        k = 1 + s * per_slot + number
        return remote(
            win.at[2 + 2 * s, rows, columns], win.at[3 + 2 * s, rows, columns],
            c_send.at[k], c_recv.at[k], {"vec": partner},
        )

    def hand_all(s):
        k = 1 + s * per_slot
        return remote(
            win.at[2 + 2 * s], win.at[3 + 2 * s], c_send.at[k], c_recv.at[k], {"vec": partner}
        )

    def d_copy(s, t):
        slot = win.at[2 + 2 * s, own_rows]
        return remote(slot, slot, d_send.at[s, t], d_recv.at[s, t], {"rep": rep_of(*direct[t])})

    def r_copy(s, t, hop, number):
        slot = win.at[2 + 2 * s, half_from(*direct[t], number % 2)]
        return remote(slot, slot, r_send.at[s, number], r_recv.at[s, number], {"rep": rep_of(*hop)})

    def relays(t):
        da, db = direct[t]
        if da == 0:
            return [((i, 0), 2 * diagonal.index((i, db))) for i in range(1, n_a)]
        return [((0, j), 2 * diagonal.index((da, j)) + 1) for j in range(1, n_b)]

    def after_z(s):
        z_copy(s).wait_recv()
        for t in range(len(direct)):
            start(d_copy(s, t))

    def after_direct(s):
        for t in range(len(direct)):
            d_copy(s, t).wait_recv()
            for hop, number in relays(t):
                start(r_copy(s, t, hop, number))

    def after_relay(s):
        for number in range(2 * len(diagonal)):
            slot = win.at[2 + 2 * s, half_from(*diagonal[number // 2], number % 2)]
            remote(
                slot, slot, r_send.at[s, number], r_recv.at[s, number], {"vec": partner}
            ).wait_recv()
        start(hand_all(s))

    def compare(slot):
        return products(scaled, win, slot, count, block_rows)

    def finish(s):
        hand_all(s).wait_recv()
        is_far, below, above = places(s, core)
        left, right = compare(2 + 2 * s)

        @pl.when(is_far == 0)
        def _():
            out_ref[below] = left

        out_ref[above] = right

    after_z(order[0])
    start(rows_partner)
    loop(lambda i: rows_out(i).start())
    after_z(order[1])
    after_direct(order[0])
    after_z(order[2])
    after_direct(order[1])

    def pass_rows(i):
        rows_out(i).wait_recv()
        rows_across(i).start()

    loop(pass_rows)
    after_direct(order[2])
    after_relay(order[0])

    rows_partner.wait_recv()
    loop(lambda i: rows_across(i).wait_recv())
    pivots = lax.fori_loop(
        0, n_vec - 1, lambda i, total: total + heard[i].astype(jnp.float32),
        rows_ref[...].astype(jnp.float32), unroll=short,
    )
    level = jnp.sum(pivots, axis=1, keepdims=True) / fields
    pivots = pivots - level
    own = win[0].astype(jnp.float32)
    for k in range(count):
        scaled[k * block_rows:(k + 1) * block_rows, :] = (own * pivots[k:k + 1, :]).astype(jnp.bfloat16)

    partner_own.wait_recv()
    left, right = compare(0)
    out_ref[HALF] = left
    out_ref[HALF + 1 - 2 * core] = right
    after_relay(order[1])
    finish(order[0])
    after_relay(order[2])
    finish(order[1])
    hand_all(order[2]).wait_recv()
    for copy in started:
        copy.wait_send()
    loop(lambda i: rows_out(i).wait_send())
    loop(lambda i: rows_across(i).wait_send())


def solution(mesh):
    n_vec, n_rep = mesh.shape["vec"], mesh.shape["rep"]
    n_b = 2 if n_rep % 2 == 0 else 1
    n_a = n_rep // n_b
    assert n_vec % 2 == 0 and n_vec > 2 * HALF

    def step(vectors, pivot_index):
        rows, fields = vectors.shape
        count = pivot_index.shape[1]
        direct = n_a + n_b - 2
        diagonal = (n_a - 1) * (n_b - 1)
        dma = pltpu.SemaphoreType.DMA
        across = 1 + 3 * (1 + direct + 2 * diagonal)
        vmem = pl.BlockSpec(memory_space=pltpu.VMEM)
        hbm = pl.BlockSpec(memory_space=pltpu.HBM)
        held, win, scaled = pl.pallas_call(
            functools.partial(kernel, n_vec, n_a, n_b),
            out_shape=(
                pltpu.VMEM((2 * HALF + 1, count, rows, rows), jnp.bfloat16),
                pltpu.VMEM((8, rows, fields), jnp.bfloat16),
                pltpu.VMEM((count * rows, fields), jnp.bfloat16),
            ),
            in_specs=[hbm, hbm],
            out_specs=(vmem, vmem, vmem),
            scratch_shapes=[
                pltpu.VMEM((1, count), jnp.int32),
                pltpu.VMEM((count, fields), jnp.bfloat16),
                pltpu.VMEM((n_vec - 1, count, fields), jnp.bfloat16),
                dma((3,)), dma((3,)),
                dma((3, max(direct, 1))), dma((3, max(direct, 1))),
                dma((3, max(2 * diagonal, 1))), dma((3, max(2 * diagonal, 1))),
                dma((n_vec - 1,)), dma((n_vec - 1,)),
                dma((across,)), dma((across,)),
                dma((2,)),
            ],
            compiler_params=pltpu.CompilerParams(
                collective_id=0, has_side_effects=True, vmem_limit_bytes=60_800_000
            ),
        )(vectors, pivot_index)
        return pl.pallas_call(
            functools.partial(closing, n_vec),
            out_shape=jax.ShapeDtypeStruct(held.shape, held.dtype),
            in_specs=[vmem, vmem, vmem],
            out_specs=pl.BlockSpec(memory_space=pl.ANY),
            scratch_shapes=[
                pltpu.VMEM((2, *held.shape[1:]), held.dtype), dma((2 * HALF + 3,)),
            ],
            compiler_params=pltpu.CompilerParams(vmem_limit_bytes=24 * 2**20),
        )(held, win, scaled)

    return jax.shard_map(
        step, mesh=mesh, in_specs=(P("vec", None), P("rep", None)),
        out_specs=P(None, "rep", "vec", None), check_vma=False,
    )
```

profile of v0, /device:TPU:0, one launch (start us, length us, event | category | flops | bytes accessed | tf_op | source)
XLA Modules:
  0.0 25.2 jit_solution(12531760314797311370)
XLA Ops:
  0.0 23.2 %shard_map.28 = (bf16[7,8,128,128]{3,2,1,0:T(8,128)(2,1)S(1)}, bf16[8,128,1024]{2,1,0:T(8,128)(2,1)S(1)}, bf16[1024,1024]{1,0:T(8,128)(2,1)S(1)}) custom-call(bf16[128,1024]{1,0:T(8,128)(2,1)} %vec_ref.1, s32[1,8]{1,0:T(1,128)} %index_ref.1), custom_call_target="tpu_custom_call" | custom-call | tf_op jit(solution)/shard_map/pallas_call | solution.py:300
  23.2 1.9 %shard_map.29 = bf16[7,8,128,128]{3,2,1,0:T(8,128)(2,1)} custom-call(bf16[7,8,128,128]{3,2,1,0:T(8,128)(2,1)S(1)} %get-tuple-element.8.held, bf16[8,128,1024]{2,1,0:T(8,128)(2,1)S(1)} %get-tuple-element.9.win, bf16[1024,1024]{1,0:T(8,128)(2,1)S(1)} %get-tuple-element.10.scaled), custom_call_target="tpu_custom_call" | custom-call | tf_op jit(solution)/shard_map/pallas_call | solution.py:324
where the time goes:
time: 25.3 us; the launch traced here: 25.2 us
  Pallas kernels  25.2 us (100%)
    pallas_call x1, Pallas kernels, step(): pl.pallas_call(functools.partial(kernel, n_vec, n_a, n_b), out_shape=(plt...  23.2 us
    pallas_call x1, Pallas kernels, step(): pl.pallas_call(functools.partial(closing, n_vec), out_shape=jax.ShapeDtyp...  1.95 us

commit v1 on v0

v1 whole, which is shorter than its diff:
```python
import functools
import math

import jax
import jax.numpy as jnp
from jax import lax
from jax.experimental import pallas as pl
from jax.experimental.pallas import tpu as pltpu
from jax.sharding import PartitionSpec as P

HALF = 3
NEAR, OUTER, FAR = 0, 1, 2


def contract(left, right):
    return lax.dot_general(
        left, right, (((1,), (1,)), ((), ())), preferred_element_type=jnp.float32
    )


def inward(chip, chips):
    return 1 - 2 * (2 * chip // chips) if chips <= 4 else 1 + 0 * chip


def place(slot, core, way):
    if slot == FAR:
        return 2 * HALF * core
    step = way if slot == NEAR else -way
    return HALF + 2 * step, HALF + 2 * step + 1 - 2 * core


def products(scaled, right, count):
    fields = scaled.shape[1]
    value = (contract(scaled, right) * (1.0 / math.sqrt(fields))).astype(jnp.bfloat16)
    return value.reshape(count, scaled.shape[0] // count, right.shape[0])


def closing(n_vec, held, win, scaled, out_ref, last, sems):
    window, count, block_rows, _ = held.shape
    core = lax.axis_index("vec") % 2
    spot = place(FAR, core, 1)

    def ready(i):
        return pltpu.make_async_copy(held.at[i], out_ref.at[i], sems.at[i])

    late = pltpu.make_async_copy(last, out_ref.at[spot], sems.at[window])
    for i in range(window):
        pl.when(spot != i)(lambda i=i: ready(i).start())
    last[...] = products(scaled[...], win[6], count)
    late.start()
    for i in range(window):
        pl.when(spot != i)(lambda i=i: ready(i).wait())
    late.wait()


def kernel(
    n_vec, n_a, n_b, vec_ref, index_ref, out_ref, win, scaled, wanted_ref, rows_ref, heard,
    z_send, z_recv, f_send, f_recv, d_send, d_recv, r_send, r_recv, p_send, p_recv,
    h_send, h_recv, o_send, o_recv, local_sem, allow,
):
    block_rows, fields = vec_ref.shape
    count = index_ref.shape[1]
    n_rep = n_a * n_b
    chips = n_vec // 2
    part = block_rows // n_rep
    piece = part // 2
    me = lax.axis_index("vec")
    rep = lax.axis_index("rep")
    a, b = rep // n_b, rep % n_b
    chip, core = me // 2, me % 2
    partner = {"vec": me + 1 - 2 * core}
    way = inward(chip, chips)
    short = n_vec <= 16

    def at_chip(offset, which):
        return {"vec": 2 * ((chip + offset + chips) % chips) + which}

    def rep_of(da, db):
        return ((a + da + n_a) % n_a) * n_b + (b + db + n_b) % n_b

    direct = [(0, i) for i in range(1, n_b)] + [(i, 0) for i in range(1, n_a)]
    diagonal = [(i, j) for i in range(1, n_a) for j in range(1, n_b)]
    relays = {}
    for t, (da, db) in enumerate(direct):
        if da == 0:
            relays[t] = [((i, 0), diagonal.index((i, db))) for i in range(1, n_a)]
        else:
            relays[t] = [((0, j), diagonal.index((da, j))) for j in range(1, n_b)]
    side = [0 if da == 0 else 1 for da, _ in direct]

    own_copy = pltpu.make_async_copy(vec_ref, win.at[0], local_sem.at[0])
    index_copy = pltpu.make_async_copy(index_ref, wanted_ref, local_sem.at[1])
    own_copy.start()
    index_copy.start()

    def chip_index(offset):
        return (chip + offset + chips) % chips

    def is_up(offset):
        return chip_index(offset) > chip

    def rep_is_up(da, db):
        return rep_of(da, db) > rep

    def number_of(flags):
        return sum(flag.astype(jnp.int32) for flag in flags)

    def everywhere(action):
        def body(i, carry):
            action(i)
            return carry

        lax.fori_loop(1, chips, body, 0, unroll=short)

    barrier = pltpu.get_barrier_semaphore()

    def meet(sem, when, device):
        pl.when(when)(lambda: pl.semaphore_signal(sem, inc=1, device_id=device))

    sides = (1, -1)
    everywhere(lambda i: meet(barrier, is_up(i), at_chip(i, core)))
    for step in sides:
        meet(barrier, is_up(step), at_chip(step, 1 - core))
    for hop in direct:
        meet(barrier, rep_is_up(*hop), {"rep": rep_of(*hop)})
    pl.semaphore_signal(barrier, inc=1, device_id=partner)
    ups = number_of([is_up(step) for step in sides])
    rep_ups = number_of([rep_is_up(*hop) for hop in direct]) if direct else jnp.int32(0)
    pl.semaphore_wait(barrier, chip + (2 - ups) + (len(direct) - rep_ups) + 1)
    meet(allow.at[0], jnp.logical_not(is_up(-1)), at_chip(-1, core))
    everywhere(lambda i: meet(allow.at[1], jnp.logical_not(is_up(i)), at_chip(i, core)))
    for hop in direct:
        meet(allow.at[2], jnp.logical_not(rep_is_up(*hop)), {"rep": rep_of(*hop)})
    for step in sides:
        meet(allow.at[3], jnp.logical_not(is_up(step)), at_chip(step, 1 - core))

    def allowed(i, times):
        pl.when(times > 0)(lambda: pl.semaphore_wait(allow.at[i], times))

    def remote(src, dst, send_sem, recv_sem, device):
        return pltpu.make_async_remote_copy(
            src_ref=src, dst_ref=dst, send_sem=send_sem, recv_sem=recv_sem, device_id=device
        )

    sent = []

    def start(make, *args):
        make(*args).start()
        sent.append((make, args))

    def rows_at(which, h):
        return pl.ds(pl.multiple_of(which * part + h * piece, piece), piece)

    def quarter(da, db, h):
        return rows_at(rep_of(-da, -db), h)

    own = [rows_at(rep, h) for h in range(2)]

    def z_copy(step, h):
        target = (chip + step + chips) % chips
        slot = (1 - step * inward(target, chips) * -1) // 2
        return remote(
            vec_ref.at[own[h]], win.at[2 + 2 * slot, own[h]], z_send.at[(1 - step) // 2, h],
            z_recv.at[slot, h], at_chip(step, core),
        )

    def z_arrival(slot, h):
        spot = win.at[2 + 2 * slot, own[h]]
        return remote(spot, spot, z_send.at[0, 0], z_recv.at[slot, h], partner)

    def rows_out(i):
        return remote(rows_ref, heard.at[i], p_send.at[i], p_recv.at[i], at_chip(i, core))

    rows_partner = remote(rows_ref, heard.at[0], p_send.at[0], p_recv.at[0], partner)

    def rows_across(i):
        k = chips - 1 + i
        return remote(heard.at[i], heard.at[k], p_send.at[k], p_recv.at[k], partner)

    def passes(slot):
        if chips <= 4:
            return jnp.logical_and(chip != 0, chip != chips - 1)
        return core == slot

    def pass_on(slot, h):
        step = -way if slot == NEAR else way
        return remote(
            win.at[2 + 2 * slot, own[h]], win.at[6, own[h]], f_send.at[slot, h], f_recv.at[h],
            at_chip(step, 1 - core),
        )

    def far_arrival(h):
        spot = win.at[6, own[h]]
        return remote(spot, spot, f_send.at[0, 0], f_recv.at[h], partner)

    def d_copy(slot, t, h):
        spot = win.at[2 + 2 * slot, own[h]]
        return remote(spot, spot, d_send.at[slot, t, h], d_recv.at[slot, t, h], {"rep": rep_of(*direct[t])})

    def r_copy(slot, t, hop, number):
        spot = win.at[2 + 2 * slot, quarter(*direct[t], side[t])]
        k = 2 * number + side[t]
        return remote(spot, spot, r_send.at[slot, k], r_recv.at[slot, k], {"rep": rep_of(*hop)})

    hands = [0, 0]

    def hand(slot, rows):
        if slot == FAR:
            return
        k = hands[slot]
        hands[slot] += 1
        start(lambda: remote(
            win.at[2 + 2 * slot, rows()], win.at[3 + 2 * slot, rows()], h_send.at[slot, k],
            h_recv.at[slot], partner,
        ))

    def handed(slot):
        spot = win.at[3 + 2 * slot]
        remote(spot, spot, h_send.at[slot, 0], h_recv.at[slot], partner).wait_recv()

    def first(slot, h):
        (far_arrival(h) if slot == FAR else z_arrival(slot, h)).wait_recv()
        for t in range(len(direct)):
            start(d_copy, slot, t, h)
        hand(slot, lambda: own[h])

    def second(slot, h):
        for t in range(len(direct)):
            d_copy(slot, t, h).wait_recv()
            if side[t] == h:
                for hop, number in relays[t]:
                    start(r_copy, slot, t, hop, number)
            hand(slot, lambda t=t: quarter(*direct[t], h))

    def third(slot):
        for number in range(len(diagonal)):
            for h in range(2):
                spot = win.at[2 + 2 * slot, quarter(*diagonal[number], h)]
                k = 2 * number + h
                remote(spot, spot, r_send.at[slot, k], r_recv.at[slot, k], partner).wait_recv()
                hand(slot, lambda number=number, h=h: quarter(*diagonal[number], h))

    partner_own = remote(vec_ref, win.at[1], o_send.at[0], o_recv.at[0], partner)

    def scope(name, action, *args):
        with jax.named_scope(name):
            return action(*args)

    def prepare():
        pivots = lax.fori_loop(
            0, n_vec - 1, lambda i, total: total + heard[i].astype(jnp.float32),
            rows_ref[...].astype(jnp.float32), unroll=short,
        )
        level = jnp.sum(pivots, axis=1, keepdims=True) / fields
        pivots = pivots - level
        block = win[0].astype(jnp.float32)
        for k in range(count):
            scaled[k * block_rows:(k + 1) * block_rows, :] = (block * pivots[k:k + 1, :]).astype(jnp.bfloat16)

    def compare(i):
        step = way * (i % 2) - way * (i // 2)
        mine_at = HALF + 2 * step
        other_at = mine_at + 1 - 2 * core
        value = products(scaled[...], win[pl.ds(2 * i, 2)].reshape(2 * block_rows, fields), count)
        out_ref[mine_at] = value[:, :, :block_rows]
        out_ref[other_at] = value[:, :, block_rows:]

    lower = jnp.logical_not
    for h in range(2):
        for step in (-1, 1):
            pl.when(lower(is_up(step)))(lambda: z_copy(step, h).start())
    partner_own.start()

    index_copy.wait()
    own_copy.wait()
    wanted = wanted_ref[...] - me * block_rows
    spots = lax.broadcasted_iota(jnp.int32, (block_rows, count), 0)
    onehot = (spots == wanted).astype(jnp.bfloat16)
    mine = lax.dot_general(
        onehot, win[0], (((0,), (0,)), ((), ())), preferred_element_type=jnp.float32
    )
    rows_ref[...] = mine.astype(jnp.bfloat16)
    rows_partner.start()
    everywhere(lambda i: pl.when(lower(is_up(i)))(lambda: rows_out(i).start()))

    @pl.when(is_up(1))
    def _():
        pl.semaphore_wait(allow.at[0], 1)
        for h in range(2):
            z_copy(1, h).start()

    def pass_rows(i):
        rows_out(i).wait_recv()
        rows_across(i).start()

    allowed(2, rep_ups)
    scope("z00", first, NEAR, 0)
    scope("z01", first, NEAR, 1)
    allowed(3, ups)
    allowed(1, chips - 1 - chip)
    for h in range(2):
        pl.when(is_up(-1))(lambda: z_copy(-1, h).start())
    everywhere(lambda i: pl.when(is_up(i))(lambda: rows_out(i).start()))
    for h in range(2):
        pl.when(passes(NEAR))(lambda: pass_on(NEAR, h).start())
    scope("z10", first, OUTER, 0)
    scope("z11", first, OUTER, 1)
    for h in range(2):
        pl.when(passes(OUTER))(lambda: pass_on(OUTER, h).start())
    scope("d00", second, NEAR, 0)
    scope("d01", second, NEAR, 1)
    scope("z20", first, FAR, 0)
    scope("z21", first, FAR, 1)
    scope("passrows", everywhere, pass_rows)
    scope("d10", second, OUTER, 0)
    scope("d11", second, OUTER, 1)
    scope("r0", third, NEAR)
    scope("d20", second, FAR, 0)
    scope("d21", second, FAR, 1)
    scope("rp", rows_partner.wait_recv)
    scope("ra", everywhere, lambda i: rows_across(i).wait_recv())
    scope("scaled", prepare)
    scope("po", partner_own.wait_recv)

    def body(i, carry):
        @pl.when(i == 1)
        def _():
            scope("r1", third, OUTER)
            scope("h0", handed, NEAR)

        pl.when(i == 2)(lambda: scope("h1", handed, OUTER))
        scope("cmp", compare, i)
        return carry

    lax.fori_loop(0, 3, body, 0)
    scope("r2", third, FAR)
    with jax.named_scope("drain"):
        for make, args in sent:
            make(*args).wait_send()
        for h in range(2):
            for step in sides:
                z_copy(step, h).wait_send()
        for slot in (NEAR, OUTER):
            for h in range(2):
                pl.when(passes(slot))(lambda: pass_on(slot, h).wait_send())
        rows_partner.wait_send()
        partner_own.wait_send()
        everywhere(lambda i: rows_out(i).wait_send())
        everywhere(lambda i: rows_across(i).wait_send())


def solution(mesh):
    n_vec, n_rep = mesh.shape["vec"], mesh.shape["rep"]
    n_b = 2 if n_rep % 2 == 0 else 1
    n_a = n_rep // n_b
    assert n_vec % 2 == 0 and n_vec > 2 * HALF

    def step(vectors, pivot_index):
        rows, fields = vectors.shape
        count = pivot_index.shape[1]
        direct = max(n_a + n_b - 2, 1)
        diagonal = max((n_a - 1) * (n_b - 1), 1)
        dma = pltpu.SemaphoreType.DMA
        vmem = pl.BlockSpec(memory_space=pltpu.VMEM)
        hbm = pl.BlockSpec(memory_space=pltpu.HBM)
        held, win, scaled = pl.pallas_call(
            functools.partial(kernel, n_vec, n_a, n_b),
            out_shape=(
                pltpu.VMEM((2 * HALF + 1, count, rows, rows), jnp.bfloat16),
                pltpu.VMEM((7, rows, fields), jnp.bfloat16),
                pltpu.VMEM((count * rows, fields), jnp.bfloat16),
            ),
            in_specs=[hbm, hbm],
            out_specs=(vmem, vmem, vmem),
            scratch_shapes=[
                pltpu.VMEM((1, count), jnp.int32),
                pltpu.VMEM((count, fields), jnp.bfloat16),
                pltpu.VMEM((n_vec - 1, count, fields), jnp.bfloat16),
                dma((2, 2)), dma((2, 2)),
                dma((2, 2)), dma((2,)),
                dma((3, direct, 2)), dma((3, direct, 2)),
                dma((3, 2 * diagonal)), dma((3, 2 * diagonal)),
                dma((n_vec - 1,)), dma((n_vec - 1,)),
                dma((2, 2 * (1 + direct + diagonal))), dma((2,)),
                dma((1,)), dma((1,)),
                dma((2,)), pltpu.SemaphoreType.REGULAR((4,)),
            ],
            compiler_params=pltpu.CompilerParams(
                collective_id=0, has_side_effects=True, vmem_limit_bytes=60_800_000
            ),
        )(vectors, pivot_index)
        return pl.pallas_call(
            functools.partial(closing, n_vec),
            out_shape=jax.ShapeDtypeStruct(held.shape, held.dtype),
            in_specs=[vmem, vmem, vmem],
            out_specs=pl.BlockSpec(memory_space=pl.ANY),
            scratch_shapes=[pltpu.VMEM(held.shape[1:], held.dtype), dma((2 * HALF + 2,))],
            compiler_params=pltpu.CompilerParams(vmem_limit_bytes=24 * 2**20),
        )(held, win, scaled)

    return jax.shard_map(
        step, mesh=mesh, in_specs=(P("vec", None), P("rep", None)),
        out_specs=P(None, "rep", "vec", None), check_vma=False,
    )
```

time: 25.3 us -> 21.9 us (0.87)
  Pallas kernels: 25.2 us -> 21.7 us
    pallas_call x1, Pallas kernels: 23.2 us -> 19.8 us  [step(): pl.pallas_call(functools.partial(kernel, n_vec, n_a, n_b), out_shape=(plt...]
where the time goes in v1:
time: 21.9 us; the launch traced here: 21.7 us
  Pallas kernels  21.7 us (99%)
    pallas_call x1, Pallas kernels, step(): pl.pallas_call(functools.partial(kernel, n_vec, n_a, n_b), out_shape=(plt...  19.8 us
    pallas_call x1, Pallas kernels, step(): pl.pallas_call(functools.partial(closing, n_vec), out_shape=jax.ShapeDtyp...  1.88 us

profile of v1, /device:TPU:0, one launch (start us, length us, event | category | flops | bytes accessed | tf_op | source)
XLA Modules:
  0.0 21.7 jit_solution(14526773771501374347)
XLA Ops:
  0.0 19.8 %shard_map.28 = (bf16[7,8,128,128]{3,2,1,0:T(8,128)(2,1)S(1)}, bf16[7,128,1024]{2,1,0:T(8,128)(2,1)S(1)}, bf16[1024,1024]{1,0:T(8,128)(2,1)S(1)}) custom-call(bf16[128,1024]{1,0:T(8,128)(2,1)} %vec_ref.1, s32[1,8]{1,0:T(1,128)} %index_ref.1), custom_call_target="tpu_custom_call" | custom-call | tf_op jit(solution)/shard_map/pallas_call | solution.py:366
  19.8 1.9 %shard_map.29 = bf16[7,8,128,128]{3,2,1,0:T(8,128)(2,1)} custom-call(bf16[7,8,128,128]{3,2,1,0:T(8,128)(2,1)S(1)} %get-tuple-element.8.held, bf16[7,128,1024]{2,1,0:T(8,128)(2,1)S(1)} %get-tuple-element.9.win, bf16[1024,1024]{1,0:T(8,128)(2,1)S(1)} %get-tuple-element.10.scaled), custom_call_target="tpu_custom_call" | custom-call | tf_op jit(solution)/shard_map/pallas_call | solution.py:392

commit v2 on v1

v2 whole, which is shorter than its diff:
```python
import functools
import math

import jax
import jax.numpy as jnp
from jax import lax
from jax.experimental import pallas as pl
from jax.experimental.pallas import tpu as pltpu
from jax.sharding import PartitionSpec as P

HALF = 3
NEAR, OUTER, FAR = 0, 1, 2
AT = (3, 5, 2)
LAST = FAR
RELAY, ROUTED, WIDE = range(3)
EDGE, AMID, RING, HEAD = range(4)
def words(*parts):
    return " ".join(parts)


MODES = ((RELAY, WIDE, ROUTED), (RELAY, WIDE, RELAY), (RELAY, RELAY, RELAY))
STEPS = {
    HEAD: (words("z00 z01 up outward", "inward z10 d00 d01", "z11 z20 z21 rows"), words("r0 d10 d11 r1", "h0"), words("d20 d21 h1"), words("r2")),
    EDGE: (words("z00 z01 up outward", "inward z10 d00 d01", "z11 z20 z21 rows"), words("r0 d10 d11 d20", "d21 r1 h0"), words("h1"), words("r2")),
    AMID: (words("z00 z10 z11 z01", "up outward d00 d01", "z20 z21 r1 d10", "d11 rows"), words("h1 r0 d20 d21"), words("h0"), words("r2")),
    RING: (words("z00 z10 z01 z11", "up d00 d01 rows", "z20 z21 d10 d11", "r0 d20 d21 r1"), words("h0"), words("h1"), words("r2")),
}
CHUNKS = 1
SWAP = True


def contract(left, right):
    return lax.dot_general(
        left, right, (((1,), (1,)), ((), ())), preferred_element_type=jnp.float32
    )


def inward(chip, chips):
    return 1 - 2 * (2 * chip // chips) if chips <= 4 else 1 + 0 * chip


def pairs(i, core, way):
    if isinstance(i, int) and i == 3 and LAST == FAR:
        return 1, HALF + 1 - 2 * core, 2 * HALF * core
    if isinstance(i, int) and i == 3:
        return 5, HALF - 2 * way, HALF - 2 * way + 1 - 2 * core
    if LAST == FAR:
        step = way * (i % 2) - way * (i // 2)
        mine = HALF + 2 * step
        return (i > 0) + 2 * i, mine, mine + 1 - 2 * core
    near, far = i % 2, i // 2
    mine = HALF + 2 * way * near + far * (1 - 2 * core)
    other = (HALF + 2 * way * near + 1 - 2 * core) * (1 - far) + 2 * HALF * core * far
    return 3 * near + far, mine, other


def products(scaled, right, count):
    value = (contract(scaled, right) * (1.0 / math.sqrt(scaled.shape[1]))).astype(jnp.bfloat16)
    return value.reshape(count, scaled.shape[0] // count, right.shape[0])


def closing(n_vec, held, win, scaled, out_ref, last, sems):
    window, count, block_rows, fields = held.shape[0], held.shape[1], held.shape[2], win.shape[2]
    me = lax.axis_index("vec")
    base, first, second = pairs(3, me % 2, inward(me // 2, n_vec // 2))
    fresh = [second] if LAST == FAR else [first, second]

    def ready(i):
        return pltpu.make_async_copy(held.at[i], out_ref.at[i], sems.at[i, 0])

    some = count // CHUNKS

    def late(j, n):
        ks = pl.ds(n * some, some)
        return pltpu.make_async_copy(last.at[j, ks], out_ref.at[fresh[j], ks], sems.at[window + j, n])

    def others(action):
        for i in range(window):
            unlike = fresh[0] != i
            for spot in fresh[1:]:
                unlike = jnp.logical_and(unlike, spot != i)
            pl.when(unlike)(lambda i=i: action(i))

    with jax.named_scope("s"):
        others(lambda i: ready(i).start())
    right = win[base:base + 2].reshape(2 * block_rows, fields)
    for n in range(CHUNKS):
        with jax.named_scope(f"c{n}"):
            value = products(scaled[n * some * block_rows:(n + 1) * some * block_rows], right, some)
            for j in range(len(fresh)):
                h = 2 - len(fresh) + j
                last[j, n * some:(n + 1) * some] = value[:, :, h * block_rows:(h + 1) * block_rows]
                late(j, n).start()
    with jax.named_scope("w0"):
        others(lambda i: ready(i).wait())
    with jax.named_scope("w1"):
        for j in range(len(fresh)):
            for n in range(CHUNKS):
                late(j, n).wait()


def kernel(
    n_vec, n_a, n_b, vec_ref, index_ref, out_ref, win, scaled, wanted_ref, rows_ref, chip_ref, heard,
    out_sem, z_recv, f_recv, d_recv, r_recv, p_recv, h_recv, o_recv, local_sem, allow,
):
    block_rows, fields = vec_ref.shape
    count = index_ref.shape[1]
    n_rep = n_a * n_b
    chips = n_vec // 2
    part = block_rows // n_rep
    piece = part // 2
    me = lax.axis_index("vec")
    rep = lax.axis_index("rep")
    a, b = rep // n_b, rep % n_b
    chip, core = me // 2, me % 2
    partner = {"vec": me + 1 - 2 * core}
    way = inward(chip, chips)
    short = n_vec <= 16

    def chip_index(offset):
        return (chip + offset + chips) % chips

    def at_chip(offset, which):
        return {"vec": 2 * chip_index(offset) + which}

    def rep_of(da, db):
        return ((a + da + n_a) % n_a) * n_b + (b + db + n_b) % n_b

    direct = [(0, i) for i in range(1, n_b)] + [(i, 0) for i in range(1, n_a)]
    diagonal = [(i, j) for i in range(1, n_a) for j in range(1, n_b)]
    relays = {}
    for t, (da, db) in enumerate(direct):
        if da == 0:
            relays[t] = [((i, 0), diagonal.index((i, db))) for i in range(1, n_a)]
        else:
            relays[t] = [((0, j), diagonal.index((da, j))) for j in range(1, n_b)]
    side = [0 if da == 0 else 1 for da, _ in direct]

    own_copy = pltpu.make_async_copy(vec_ref, win.at[0], local_sem.at[0])
    index_copy = pltpu.make_async_copy(index_ref, wanted_ref, local_sem.at[1])
    own_copy.start()
    index_copy.start()

    def is_up(offset):
        return chip_index(offset) > chip

    def rep_is_up(da, db):
        return rep_of(da, db) > rep

    def number_of(flags):
        return sum((flag.astype(jnp.int32) for flag in flags), jnp.int32(0))

    def everywhere(action):
        def body(i, carry):
            action(i)
            return carry

        lax.fori_loop(1, chips, body, 0, unroll=short)

    barrier = pltpu.get_barrier_semaphore()
    lower = jnp.logical_not

    def meet(sem, when, device):
        pl.when(when)(lambda: pl.semaphore_signal(sem, inc=1, device_id=device))

    def allowed(i, times):
        pl.when(times > 0)(lambda: pl.semaphore_wait(allow.at[i], times))

    sides = (1, -1)
    everywhere(lambda i: meet(barrier, is_up(i), at_chip(i, core)))
    for step in sides:
        meet(barrier, is_up(step), at_chip(step, 1 - core))
    for hop in direct:
        meet(barrier, rep_is_up(*hop), {"rep": rep_of(*hop)})
    pl.semaphore_signal(barrier, inc=1, device_id=partner)
    ups = number_of([is_up(step) for step in sides])
    rep_ups = number_of([rep_is_up(*hop) for hop in direct])
    with jax.named_scope("barrier"):
        pl.semaphore_wait(barrier, chip + (2 - ups) + (len(direct) - rep_ups) + 1)
    meet(allow.at[0], lower(is_up(-1)), at_chip(-1, core))
    everywhere(lambda i: meet(allow.at[1], lower(is_up(i)), at_chip(i, core)))
    for hop in direct:
        meet(allow.at[2], lower(rep_is_up(*hop)), {"rep": rep_of(*hop)})
    for step in sides:
        meet(allow.at[3], lower(is_up(step)), at_chip(step, 1 - core))

    def remote(src, dst, send_sem, recv_sem, device):
        return pltpu.make_async_remote_copy(
            src_ref=src, dst_ref=dst, send_sem=send_sem, recv_sem=recv_sem, device_id=device
        )

    def arrive(rows, sem):
        spot = scaled.at[pl.ds(0, rows)]
        remote(spot, spot, out_sem.at[0], sem, partner).wait_recv()

    def gone(rows):
        spot = scaled.at[pl.ds(0, rows)]
        remote(spot, spot, out_sem.at[0], o_recv.at[0], partner).wait_send()

    def rows_at(which, h):
        return pl.ds(pl.multiple_of(which * part + h * piece, piece), piece)

    def quarter(da, db, h):
        return rows_at(rep_of(-da, -db), h)

    own = [rows_at(rep, h) for h in range(2)]

    if chips <= 4:
        edge = jnp.logical_or(chip == 0, chip == chips - 1)
    else:
        edge = chip < 0

    def z_copy(step, which):
        looks = inward(chip_index(step), chips)
        slot = (1 + step * looks) // 2
        if which < 2:
            rows = own[which]
        else:
            rows = pl.ds(pl.multiple_of(rep_of(*diagonal[which - 2]) * part, part), part)
        return remote(
            vec_ref.at[rows], win.at[AT[NEAR] + (AT[OUTER] - AT[NEAR]) * slot, rows],
            out_sem.at[0], z_recv.at[slot, jnp.minimum(which, 2)], at_chip(step, core),
        )

    def passes(slot):
        return lower(edge) if chips <= 4 else core == slot

    def pass_on(slot, h):
        step = -way if slot == NEAR else way
        return remote(
            win.at[AT[slot], own[h]], win.at[AT[FAR], own[h]], out_sem.at[0], f_recv.at[h],
            at_chip(step, 1 - core),
        )

    def d_copy(slot, t, h):
        spot = win.at[AT[slot], own[h]]
        return remote(spot, spot, out_sem.at[0], d_recv.at[slot, h], {"rep": rep_of(*direct[t])})

    def routed_copy(slot, number):
        spot = win.at[AT[slot], pl.ds(pl.multiple_of(rep * part, part), part)]
        return remote(spot, spot, out_sem.at[0], r_recv.at[slot], {"rep": rep_of(*diagonal[number])})

    def r_copy(slot, t, hop):
        spot = win.at[AT[slot], quarter(*direct[t], side[t])]
        return remote(spot, spot, out_sem.at[0], r_recv.at[slot], {"rep": rep_of(*hop)})

    def hand(slot, rows):
        if slot != FAR:
            remote(
                win.at[AT[slot], rows], win.at[AT[slot] + 1, rows], out_sem.at[0], h_recv.at[slot], partner
            ).start()

    def handed(slot):
        arrive(block_rows, h_recv.at[slot])

    half = fields // 2

    def halves(src, dst, k, device):
        return remote(src, heard.at[dst], out_sem.at[1], p_recv.at[k], device)

    give_half = halves(rows_ref.at[1 - core], 0, 0, partner)
    swap = halves(chip_ref.at[1], chips, 2, partner)

    def rows_out(i):
        return halves(chip_ref.at[0], i, 1, at_chip(i, core))

    def first(slot, h, mode):
        arrive(piece, f_recv.at[h] if slot == FAR else z_recv.at[slot, h])
        if slot != FAR:
            pl.when(passes(slot))(lambda: pass_on(slot, h).start())
        for t in range(len(direct)):
            d_copy(slot, t, h).start()
        if mode == ROUTED and h == 1:
            for number in range(len(diagonal)):
                routed_copy(slot, number).start()
        hand(slot, own[h])

    def second(slot, h, mode):
        if direct:
            arrive(len(direct) * piece, d_recv.at[slot, h])
        for t in range(len(direct)):
            if side[t] == h and mode == RELAY:
                for hop, number in relays[t]:
                    r_copy(slot, t, hop).start()
            hand(slot, quarter(*direct[t], h))

    def third(slot, mode):
        if diagonal:
            arrive(len(diagonal) * part, z_recv.at[slot, 2] if mode == WIDE else r_recv.at[slot])
        for spot in diagonal:
            for h in range(2):
                hand(slot, quarter(*spot, h))

    partner_own = remote(vec_ref, win.at[1], out_sem.at[0], o_recv.at[0], partner)

    def prepare():
        mine, other = chip_ref[1].astype(jnp.float32), heard[chips].astype(jnp.float32)
        pivots = jnp.concatenate(
            [jnp.where(core == 0, mine, other), jnp.where(core == 0, other, mine)], axis=1
        )
        level = jnp.sum(pivots, axis=1, keepdims=True) / fields
        pivots = pivots - level
        block = win[0].astype(jnp.float32)
        for k in range(count):
            scaled[k * block_rows:(k + 1) * block_rows, :] = (block * pivots[k:k + 1, :]).astype(jnp.bfloat16)

    def compare(i):
        base, mine_at, other_at = pairs(i, core, way)
        value = products(scaled[...], win[pl.ds(base, 2)].reshape(2 * block_rows, fields), count)
        out_ref[mine_at] = value[:, :, :block_rows]
        out_ref[other_at] = value[:, :, block_rows:]

    def send_z(step, steps):
        for which in steps:
            z_copy(step, which).start()

    def send_wide(step):
        if diagonal:
            send_z(step, range(2, 2 + len(diagonal)))

    def extra(role):
        if role == EDGE:
            return MODES[AMID][OUTER] == WIDE, MODES[EDGE][OUTER] == WIDE
        return MODES[AMID][NEAR] == WIDE, MODES[EDGE][NEAR] == WIDE

    def up():
        allowed(1, chips - 1 - chip)
        pl.when(is_up(-1))(lambda: send_z(-1, range(2)))
        everywhere(lambda i: pl.when(is_up(i))(lambda: rows_out(i).start()))

    def add_rows():
        spot = heard.at[pl.ds(1, chips - 1)]
        remote(spot, spot, out_sem.at[1], p_recv.at[1], partner).wait_recv()
        total = lax.fori_loop(
            1, chips, lambda i, total: total + heard[i].astype(jnp.float32),
            chip_ref[0].astype(jnp.float32), unroll=short,
        )
        chip_ref[1] = total.astype(jnp.bfloat16)
        swap.start()

    def run(steps, role):
        for name in steps.split():
            slot = int(name[1]) if name[1].isdigit() else None
            with jax.named_scope(name):
                if name == "up":
                    up()
                elif name in ("inward", "outward"):
                    if extra(role)[name == "outward"]:
                        for step in sides:
                            pl.when((way == step) == (name == "inward"))(lambda: send_wide(step))
                elif name == "rows":
                    add_rows()
                elif name[0] == "z":
                    first(slot, int(name[2]), MODES[role][slot])
                elif name[0] == "d":
                    second(slot, int(name[2]), MODES[role][slot])
                elif name[0] == "r":
                    third(slot, MODES[role][slot])
                else:
                    handed(slot)

    head = jnp.logical_and(chip == 0, rep == 0)

    def by_role(i):
        if chips > 4:
            run(STEPS[RING][i], RING)
            return
        if STEPS[HEAD][i] == STEPS[EDGE][i]:
            pl.when(edge)(lambda: run(STEPS[EDGE][i], EDGE))
        else:
            pl.when(head)(lambda: run(STEPS[HEAD][i], EDGE))
            pl.when(jnp.logical_and(edge, lower(head)))(lambda: run(STEPS[EDGE][i], EDGE))
        pl.when(lower(edge))(lambda: run(STEPS[AMID][i], AMID))

    for h in range(2):
        for step in (1, -1):
            pl.when(lower(is_up(step)))(lambda: z_copy(step, h).start())
    partner_own.start()

    index_copy.wait()
    own_copy.wait()
    wanted = wanted_ref[...] - me * block_rows
    spots = lax.broadcasted_iota(jnp.int32, (block_rows, count), 0)
    onehot = (spots == wanted).astype(jnp.bfloat16)
    mine = lax.dot_general(
        onehot, win[0], (((0,), (0,)), ((), ())), preferred_element_type=jnp.float32
    )
    rows_ref[0] = mine[:, :half].astype(jnp.bfloat16)
    rows_ref[1] = mine[:, half:].astype(jnp.bfloat16)
    give_half.start()
    with jax.named_scope("half"):
        give_half.wait_recv()
    both = rows_ref[core].astype(jnp.float32) + heard[0].astype(jnp.float32)
    chip_ref[0] = both.astype(jnp.bfloat16)
    everywhere(lambda i: pl.when(lower(is_up(i)))(lambda: rows_out(i).start()))

    @pl.when(is_up(1))
    def _():
        with jax.named_scope("next"):
            pl.semaphore_wait(allow.at[0], 1)
        send_z(1, range(2))

    with jax.named_scope("allow"):
        allowed(2, rep_ups)
        allowed(3, ups)
    def body(i, carry):
        for j in range(3):
            pl.when(i == j)(lambda: by_role(j))

        @pl.when(i == 0)
        def _():
            with jax.named_scope("pivots"):
                swap.wait_recv()
                arrive(block_rows, o_recv.at[0])
            with jax.named_scope("scaled"):
                prepare()

        with jax.named_scope("cmp"):
            compare(lax.select(jnp.logical_and(lower(edge), i > 0), 3 - i, i) if chips <= 4 and SWAP else i)
        return carry

    lax.fori_loop(0, 3, body, 0)
    by_role(3)
    with jax.named_scope("drain"):
        relayed = sum(len(hops) for hops in relays.values()) * piece

        def total(role):
            rows = (3 if role == RING else 2) * part + 3 * block_rows + 3 * len(direct) * part
            for mode in MODES[role]:
                rows += relayed if mode == RELAY else len(diagonal) * part if mode == ROUTED else 0
            if role != RING:
                rows += sum(extra(role)) * len(diagonal) * part
            return rows + (2 * part if role == AMID else 0)

        if chips > 4:
            gone(total(RING))
        else:
            pl.when(edge)(lambda: gone(total(EDGE)))
            pl.when(lower(edge))(lambda: gone(total(AMID)))
        spot = heard.at[pl.ds(0, chips + 1)]
        remote(spot, spot, out_sem.at[1], p_recv.at[1], partner).wait_send()


def solution(mesh):
    n_vec, n_rep = mesh.shape["vec"], mesh.shape["rep"]
    n_b = 2 if n_rep % 2 == 0 else 1
    n_a = n_rep // n_b
    assert n_vec % 2 == 0 and n_vec > 2 * HALF

    def step(vectors, pivot_index):
        rows, fields = vectors.shape
        count = pivot_index.shape[1]
        dma = pltpu.SemaphoreType.DMA
        vmem = pl.BlockSpec(memory_space=pltpu.VMEM)
        hbm = pl.BlockSpec(memory_space=pltpu.HBM)
        held, win, scaled = pl.pallas_call(
            functools.partial(kernel, n_vec, n_a, n_b),
            out_shape=(
                pltpu.VMEM((2 * HALF + 1, count, rows, rows), jnp.bfloat16),
                pltpu.VMEM((7, rows, fields), jnp.bfloat16),
                pltpu.VMEM((count * rows, fields), jnp.bfloat16),
            ),
            in_specs=[hbm, hbm],
            out_specs=(vmem, vmem, vmem),
            scratch_shapes=[
                pltpu.VMEM((1, count), jnp.int32),
                pltpu.VMEM((2, count, fields // 2), jnp.bfloat16),
                pltpu.VMEM((2, count, fields // 2), jnp.bfloat16),
                pltpu.VMEM((n_vec // 2 + 1, count, fields // 2), jnp.bfloat16),
                dma((2,)), dma((2, 3)), dma((2,)), dma((3, 2)), dma((3,)), dma((3,)), dma((2,)),
                dma((1,)), dma((2,)), pltpu.SemaphoreType.REGULAR((4,)),
            ],
            compiler_params=pltpu.CompilerParams(
                collective_id=0, has_side_effects=True, vmem_limit_bytes=60_800_000
            ),
        )(vectors, pivot_index)
        return pl.pallas_call(
            functools.partial(closing, n_vec),
            out_shape=jax.ShapeDtypeStruct(held.shape, held.dtype),
            in_specs=[vmem, vmem, vmem],
            out_specs=pl.BlockSpec(memory_space=pl.ANY),
            scratch_shapes=[pltpu.VMEM((2, *held.shape[1:]), held.dtype), dma((2 * HALF + 3, CHUNKS))],
            compiler_params=pltpu.CompilerParams(vmem_limit_bytes=24 * 2**20),
        )(held, win, scaled)

    return jax.shard_map(
        step, mesh=mesh, in_specs=(P("vec", None), P("rep", None)),
        out_specs=P(None, "rep", "vec", None), check_vma=False,
    )
```

time: 21.9 us -> 19.2 us (0.88)
  the two profiles are of different devices: /device:TPU:0 before, /device:TPU:16 now
where the time goes in v2:
time: 19.2 us; the launch traced here: 19.1 us
  Pallas kernels  19.1 us (99%)
    pallas_call x1, Pallas kernels, step(): pl.pallas_call(functools.partial(kernel, n_vec, n_a, n_b), out_shape=(plt...  17.2 us
    pallas_call x1, Pallas kernels, step(): pl.pallas_call(functools.partial(closing, n_vec), out_shape=jax.ShapeDtyp...  1.93 us

profile of v2, /device:TPU:16, one launch (start us, length us, event | category | flops | bytes accessed | tf_op | source)
XLA Modules:
  0.0 19.1 jit_solution(6896256548547980362)
XLA Ops:
  0.0 17.2 %shard_map.28 = (bf16[7,8,128,128]{3,2,1,0:T(8,128)(2,1)S(1)}, bf16[7,128,1024]{2,1,0:T(8,128)(2,1)S(1)}, bf16[1024,1024]{1,0:T(8,128)(2,1)S(1)}) custom-call(bf16[128,1024]{1,0:T(8,128)(2,1)} %vec_ref.1, s32[1,8]{1,0:T(1,128)} %index_ref.1), custom_call_target="tpu_custom_call" | custom-call | tf_op jit(solution)/shard_map/pallas_call | solution.py:456
  17.2 1.9 %shard_map.29 = bf16[7,8,128,128]{3,2,1,0:T(8,128)(2,1)} custom-call(bf16[7,8,128,128]{3,2,1,0:T(8,128)(2,1)S(1)} %get-tuple-element.8.held, bf16[7,128,1024]{2,1,0:T(8,128)(2,1)S(1)} %get-tuple-element.9.win, bf16[1024,1024]{1,0:T(8,128)(2,1)S(1)} %get-tuple-element.10.scaled), custom_call_target="tpu_custom_call" | custom-call | tf_op jit(solution)/shard_map/pallas_call | solution.py:477

commit v3 on v2

--- a/solution.py
+++ b/solution.py
@@ -18,15 +18,16 @@
     return " ".join(parts)
 
 
-MODES = ((RELAY, WIDE, ROUTED), (RELAY, WIDE, RELAY), (RELAY, RELAY, RELAY))
+MODES = ((RELAY, WIDE, ROUTED), (RELAY, WIDE, ROUTED), (RELAY, RELAY, RELAY))
 STEPS = {
-    HEAD: (words("z00 z01 up outward", "inward z10 d00 d01", "z11 z20 z21 rows"), words("r0 d10 d11 r1", "h0"), words("d20 d21 h1"), words("r2")),
-    EDGE: (words("z00 z01 up outward", "inward z10 d00 d01", "z11 z20 z21 rows"), words("r0 d10 d11 d20", "d21 r1 h0"), words("h1"), words("r2")),
-    AMID: (words("z00 z10 z11 z01", "up outward d00 d01", "z20 z21 r1 d10", "d11 rows"), words("h1 r0 d20 d21"), words("h0"), words("r2")),
+    HEAD: (words("up z00 z01 inward", "outward z10 d00 d01", "z11 z20 z21 rows"), words("r0 d10 d11 r1", "h0"), words("h1"), words("d20 d21 r2")),
+    EDGE: (words("up z00 z01 inward", "outward z10 d00 d01", "z11 z20 z21 rows"), words("r0 d10 d11 r1", "h0"), words("h1"), words("d20 d21 r2")),
+    AMID: (words("up z00 z10 z11", "z01 outward d00 d01", "z20 z21 r1 d10", "d11 rows"), words("h1"), words("r0 h0"), words("d20 d21 r2")),
     RING: (words("z00 z10 z01 z11", "up d00 d01 rows", "z20 z21 d10 d11", "r0 d20 d21 r1"), words("h0"), words("h1"), words("r2")),
 }
 CHUNKS = 1
 SWAP = True
+SIDES = (-1, 1)
 
 
 def contract(left, right):
@@ -236,8 +237,8 @@
         spot = win.at[AT[slot], own[h]]
         return remote(spot, spot, out_sem.at[0], d_recv.at[slot, h], {"rep": rep_of(*direct[t])})
 
-    def routed_copy(slot, number):
-        spot = win.at[AT[slot], pl.ds(pl.multiple_of(rep * part, part), part)]
+    def routed_copy(slot, number, h):
+        spot = win.at[AT[slot], own[h]]
         return remote(spot, spot, out_sem.at[0], r_recv.at[slot], {"rep": rep_of(*diagonal[number])})
 
     def r_copy(slot, t, hop):
@@ -268,11 +269,11 @@
         arrive(piece, f_recv.at[h] if slot == FAR else z_recv.at[slot, h])
         if slot != FAR:
             pl.when(passes(slot))(lambda: pass_on(slot, h).start())
+        if mode == ROUTED:
+            for number in range(len(diagonal)):
+                routed_copy(slot, number, h).start()
         for t in range(len(direct)):
             d_copy(slot, t, h).start()
-        if mode == ROUTED and h == 1:
-            for number in range(len(diagonal)):
-                routed_copy(slot, number).start()
         hand(slot, own[h])
 
     def second(slot, h, mode):
@@ -373,7 +374,7 @@
         pl.when(lower(edge))(lambda: run(STEPS[AMID][i], AMID))
 
     for h in range(2):
-        for step in (1, -1):
+        for step in SIDES:
             pl.when(lower(is_up(step)))(lambda: z_copy(step, h).start())
     partner_own.start()
 

time: 19.2 us -> 18.6 us (0.969)
  the two profiles are of different devices: /device:TPU:16 before, /device:TPU:0 now
where the time goes in v3:
time: 18.6 us; the launch traced here: 18.5 us
  Pallas kernels  18.5 us (99%)
    pallas_call x1, Pallas kernels, step(): pl.pallas_call(functools.partial(kernel, n_vec, n_a, n_b), out_shape=(plt...  16.5 us
    pallas_call x1, Pallas kernels, step(): pl.pallas_call(functools.partial(closing, n_vec), out_shape=jax.ShapeDtyp...  1.92 us

profile of v3, /device:TPU:0, one launch (start us, length us, event | category | flops | bytes accessed | tf_op | source)
XLA Modules:
  0.0 18.5 jit_solution(4089161298830529183)
XLA Ops:
  0.0 16.5 %shard_map.28 = (bf16[7,8,128,128]{3,2,1,0:T(8,128)(2,1)S(1)}, bf16[7,128,1024]{2,1,0:T(8,128)(2,1)S(1)}, bf16[1024,1024]{1,0:T(8,128)(2,1)S(1)}) custom-call(bf16[128,1024]{1,0:T(8,128)(2,1)} %vec_ref.1, s32[1,8]{1,0:T(1,128)} %index_ref.1), custom_call_target="tpu_custom_call" | custom-call | tf_op jit(solution)/shard_map/pallas_call | solution.py:457
  16.6 1.9 %shard_map.29 = bf16[7,8,128,128]{3,2,1,0:T(8,128)(2,1)} custom-call(bf16[7,8,128,128]{3,2,1,0:T(8,128)(2,1)S(1)} %get-tuple-element.8.held, bf16[7,128,1024]{2,1,0:T(8,128)(2,1)S(1)} %get-tuple-element.9.win, bf16[1024,1024]{1,0:T(8,128)(2,1)S(1)} %get-tuple-element.10.scaled), custom_call_target="tpu_custom_call" | custom-call | tf_op jit(solution)/shard_map/pallas_call | solution.py:478

commit v4 on v3

--- a/solution.py
+++ b/solution.py
@@ -13,18 +13,54 @@
 AT = (3, 5, 2)
 LAST = FAR
 RELAY, ROUTED, WIDE = range(3)
-EDGE, AMID, RING, HEAD = range(4)
+LOW_END, LOW_MID, HIGH_MID, HIGH_END, RING = range(5)
+ACROSS = (HIGH_END, HIGH_MID, LOW_MID, LOW_END)
+BESIDE = (LOW_MID, LOW_END, HIGH_END, HIGH_MID)
+MODES = (
+    (RELAY, WIDE, WIDE),
+    (WIDE, WIDE, ROUTED),
+    (RELAY, WIDE, ROUTED),
+    (RELAY, WIDE, ROUTED),
+    (RELAY, RELAY, RELAY),
+)
+
+
 def words(*parts):
     return " ".join(parts)
 
 
-MODES = ((RELAY, WIDE, ROUTED), (RELAY, WIDE, ROUTED), (RELAY, RELAY, RELAY))
-STEPS = {
-    HEAD: (words("up z00 z01 inward", "outward z10 d00 d01", "z11 z20 z21 rows"), words("r0 d10 d11 r1", "h0"), words("h1"), words("d20 d21 r2")),
-    EDGE: (words("up z00 z01 inward", "outward z10 d00 d01", "z11 z20 z21 rows"), words("r0 d10 d11 r1", "h0"), words("h1"), words("d20 d21 r2")),
-    AMID: (words("up z00 z10 z11", "z01 outward d00 d01", "z20 z21 r1 d10", "d11 rows"), words("h1"), words("r0 h0"), words("d20 d21 r2")),
-    RING: (words("z00 z10 z01 z11", "up d00 d01 rows", "z20 z21 d10 d11", "r0 d20 d21 r1"), words("h0"), words("h1"), words("r2")),
-}
+STEPS = (
+    (
+        words("up z00 z01 inward", "outward z10 d00 d01", "z11 z20 z21 rows"),
+        words("r0 d10 d11 r1", "h0"),
+        words("h1"),
+        words("d20 d21 r2"),
+    ),
+    (
+        words("up z00 z10 z11", "z01 d00 d01 r0", "z20 z21 r1 d10", "d11 rows"),
+        words("h1"),
+        words("h0"),
+        words("d20 d21 r2"),
+    ),
+    (
+        words("up inward z00 z10", "z11 z01 d00 d01", "z20 z21 r1 d10", "d11 rows"),
+        words("h1"),
+        words("r0 h0"),
+        words("d20 d21 r2"),
+    ),
+    (
+        words("up z00 z01 inward", "outward z10 d00 d01", "z11 z20 z21 rows"),
+        words("r0 d10 d11 r1", "h0"),
+        words("h1"),
+        words("d20 d21 r2"),
+    ),
+    (
+        words("z00 z10 z01 z11", "up d00 d01 rows", "z20 z21 d10 d11", "r0 d20 d21 r1"),
+        words("h0"),
+        words("h1"),
+        words("r2"),
+    ),
+)
 CHUNKS = 1
 SWAP = True
 SIDES = (-1, 1)
@@ -37,7 +73,7 @@
 
 
 def inward(chip, chips):
-    return 1 - 2 * (2 * chip // chips) if chips <= 4 else 1 + 0 * chip
+    return 1 - 2 * (2 * chip // chips) if chips == 4 else 1 + 0 * chip
 
 
 def pairs(i, core, way):
@@ -206,7 +242,7 @@
 
     own = [rows_at(rep, h) for h in range(2)]
 
-    if chips <= 4:
+    if chips == 4:
         edge = jnp.logical_or(chip == 0, chip == chips - 1)
     else:
         edge = chip < 0
@@ -224,7 +260,7 @@
         )
 
     def passes(slot):
-        return lower(edge) if chips <= 4 else core == slot
+        return lower(edge) if chips == 4 else core == slot
 
     def pass_on(slot, h):
         step = -way if slot == NEAR else way
@@ -285,9 +321,20 @@
                     r_copy(slot, t, hop).start()
             hand(slot, quarter(*direct[t], h))
 
-    def third(slot, mode):
+    def third(slot, mode, role):
         if diagonal:
-            arrive(len(diagonal) * part, z_recv.at[slot, 2] if mode == WIDE else r_recv.at[slot])
+            if mode != WIDE:
+                sem = r_recv.at[slot]
+            else:
+                sem = f_recv.at[2] if slot == FAR else z_recv.at[slot, 2]
+            arrive(len(diagonal) * part, sem)
+        if slot == NEAR and widens(role):
+            for spot in diagonal:
+                rows = pl.ds(pl.multiple_of(rep_of(*spot) * part, part), part)
+                remote(
+                    win.at[AT[NEAR], rows], win.at[AT[FAR], rows], out_sem.at[0], f_recv.at[2],
+                    at_chip(-way, 1 - core),
+                ).start()
         for spot in diagonal:
             for h in range(2):
                 hand(slot, quarter(*spot, h))
@@ -320,9 +367,13 @@
             send_z(step, range(2, 2 + len(diagonal)))
 
     def extra(role):
-        if role == EDGE:
-            return MODES[AMID][OUTER] == WIDE, MODES[EDGE][OUTER] == WIDE
-        return MODES[AMID][NEAR] == WIDE, MODES[EDGE][NEAR] == WIDE
+        ends = role in (LOW_END, HIGH_END)
+        inside = MODES[BESIDE[role]][OUTER] if ends else MODES[ACROSS[role]][NEAR]
+        outside = MODES[ACROSS[role]][OUTER] if ends else MODES[BESIDE[role]][NEAR]
+        return inside == WIDE, outside == WIDE
+
+    def widens(role):
+        return role in (LOW_MID, HIGH_MID) and MODES[BESIDE[role]][FAR] == WIDE
 
     def up():
         allowed(1, chips - 1 - chip)
@@ -356,22 +407,18 @@
                 elif name[0] == "d":
                     second(slot, int(name[2]), MODES[role][slot])
                 elif name[0] == "r":
-                    third(slot, MODES[role][slot])
+                    third(slot, MODES[role][slot], role)
                 else:
                     handed(slot)
 
-    head = jnp.logical_and(chip == 0, rep == 0)
+    is_role = [chip == 0, chip == 1, chip == 2, chip == 3]
 
     def by_role(i):
-        if chips > 4:
+        if chips != 4:
             run(STEPS[RING][i], RING)
             return
-        if STEPS[HEAD][i] == STEPS[EDGE][i]:
-            pl.when(edge)(lambda: run(STEPS[EDGE][i], EDGE))
-        else:
-            pl.when(head)(lambda: run(STEPS[HEAD][i], EDGE))
-            pl.when(jnp.logical_and(edge, lower(head)))(lambda: run(STEPS[EDGE][i], EDGE))
-        pl.when(lower(edge))(lambda: run(STEPS[AMID][i], AMID))
+        for role in range(chips):
+            pl.when(is_role[role])(lambda: run(STEPS[role][i], role))
 
     for h in range(2):
         for step in SIDES:
@@ -417,7 +464,7 @@
                 prepare()
 
         with jax.named_scope("cmp"):
-            compare(lax.select(jnp.logical_and(lower(edge), i > 0), 3 - i, i) if chips <= 4 and SWAP else i)
+            compare(lax.select(jnp.logical_and(lower(edge), i > 0), 3 - i, i) if chips == 4 and SWAP else i)
         return carry
 
     lax.fori_loop(0, 3, body, 0)
@@ -430,14 +477,14 @@
             for mode in MODES[role]:
                 rows += relayed if mode == RELAY else len(diagonal) * part if mode == ROUTED else 0
             if role != RING:
-                rows += sum(extra(role)) * len(diagonal) * part
-            return rows + (2 * part if role == AMID else 0)
-
-        if chips > 4:
+                rows += (sum(extra(role)) + widens(role)) * len(diagonal) * part
+            return rows + (2 * part if role in (LOW_MID, HIGH_MID) else 0)
+
+        if chips != 4:
             gone(total(RING))
         else:
-            pl.when(edge)(lambda: gone(total(EDGE)))
-            pl.when(lower(edge))(lambda: gone(total(AMID)))
+            for role in range(chips):
+                pl.when(is_role[role])(lambda: gone(total(role)))
         spot = heard.at[pl.ds(0, chips + 1)]
         remote(spot, spot, out_sem.at[1], p_recv.at[1], partner).wait_send()
 
@@ -468,7 +515,7 @@
                 pltpu.VMEM((2, count, fields // 2), jnp.bfloat16),
                 pltpu.VMEM((2, count, fields // 2), jnp.bfloat16),
                 pltpu.VMEM((n_vec // 2 + 1, count, fields // 2), jnp.bfloat16),
-                dma((2,)), dma((2, 3)), dma((2,)), dma((3, 2)), dma((3,)), dma((3,)), dma((2,)),
+                dma((2,)), dma((2, 3)), dma((3,)), dma((3, 2)), dma((3,)), dma((3,)), dma((2,)),
                 dma((1,)), dma((2,)), pltpu.SemaphoreType.REGULAR((4,)),
             ],
             compiler_params=pltpu.CompilerParams(

time: 18.6 us -> 18.2 us (0.978)
  the two profiles are of different devices: /device:TPU:0 before, /device:TPU:25 now
where the time goes in v4:
time: 18.2 us; the launch traced here: 18.1 us
  Pallas kernels  18.1 us (99%)
    pallas_call x1, Pallas kernels, step(): pl.pallas_call(functools.partial(kernel, n_vec, n_a, n_b), out_shape=(plt...  16.1 us
    pallas_call x1, Pallas kernels, step(): pl.pallas_call(functools.partial(closing, n_vec), out_shape=jax.ShapeDtyp...  1.93 us

profile of v4, /device:TPU:25, one launch (start us, length us, event | category | flops | bytes accessed | tf_op | source)
XLA Modules:
  0.0 18.1 jit_solution(9325796147854032617)
XLA Ops:
  0.0 16.1 %shard_map.28 = (bf16[7,8,128,128]{3,2,1,0:T(8,128)(2,1)S(1)}, bf16[7,128,1024]{2,1,0:T(8,128)(2,1)S(1)}, bf16[1024,1024]{1,0:T(8,128)(2,1)S(1)}) custom-call(bf16[128,1024]{1,0:T(8,128)(2,1)} %vec_ref.1, s32[1,8]{1,0:T(1,128)} %index_ref.1), custom_call_target="tpu_custom_call" | custom-call | tf_op jit(solution)/shard_map/pallas_call | solution.py:504
  16.1 1.9 %shard_map.29 = bf16[7,8,128,128]{3,2,1,0:T(8,128)(2,1)} custom-call(bf16[7,8,128,128]{3,2,1,0:T(8,128)(2,1)S(1)} %get-tuple-element.8.held, bf16[7,128,1024]{2,1,0:T(8,128)(2,1)S(1)} %get-tuple-element.9.win, bf16[1024,1024]{1,0:T(8,128)(2,1)S(1)} %get-tuple-element.10.scaled), custom_call_target="tpu_custom_call" | custom-call | tf_op jit(solution)/shard_map/pallas_call | solution.py:525

commit v5 on v4

--- a/solution.py
+++ b/solution.py
@@ -17,10 +17,10 @@
 ACROSS = (HIGH_END, HIGH_MID, LOW_MID, LOW_END)
 BESIDE = (LOW_MID, LOW_END, HIGH_END, HIGH_MID)
 MODES = (
-    (RELAY, WIDE, WIDE),
+    (ROUTED, WIDE, WIDE),
     (WIDE, WIDE, ROUTED),
-    (RELAY, WIDE, ROUTED),
-    (RELAY, WIDE, ROUTED),
+    (ROUTED, WIDE, ROUTED),
+    (ROUTED, WIDE, ROUTED),
     (RELAY, RELAY, RELAY),
 )
 
@@ -31,31 +31,31 @@
 
 STEPS = (
     (
-        words("up z00 z01 inward", "outward z10 d00 d01", "z11 z20 z21 rows"),
-        words("r0 d10 d11 r1", "h0"),
+        words("z00 up z01 inward", "outward corner z10 z11", "z20 z21 d00 d01", "rows r0"),
+        words("d10 d11 r1 h0"),
         words("h1"),
         words("d20 d21 r2"),
     ),
     (
-        words("up z00 z10 z11", "z01 d00 d01 r0", "z20 z21 r1 d10", "d11 rows"),
+        words("up z00 z10 z11", "z01 d00 rows d01", "corner r0 z20 z21", "r1 d10 d11"),
         words("h1"),
         words("h0"),
         words("d20 d21 r2"),
     ),
     (
-        words("up inward z00 z10", "z11 z01 d00 d01", "z20 z21 r1 d10", "d11 rows"),
+        words("up inward z00 z10", "z11 z01 corner d00", "rows d01 z20 z21", "r1 d10 d11 r0"),
         words("h1"),
-        words("r0 h0"),
+        words("h0"),
         words("d20 d21 r2"),
     ),
     (
-        words("up z00 z01 inward", "outward z10 d00 d01", "z11 z20 z21 rows"),
-        words("r0 d10 d11 r1", "h0"),
+        words("up z00 outward0 z01", "inward corner z10 outward1", "z11 z20 z21 d00", "d01 rows r0"),
+        words("d10 d11 r1 h0"),
         words("h1"),
         words("d20 d21 r2"),
     ),
     (
-        words("z00 z10 z01 z11", "up d00 d01 rows", "z20 z21 d10 d11", "r0 d20 d21 r1"),
+        words("z00 z10 z01 z11", "up d00 d01 corner", "rows z20 z21 d10", "d11 r0 d20 d21", "r1"),
         words("h0"),
         words("h1"),
         words("r2"),
@@ -205,21 +205,26 @@
 
     sides = (1, -1)
     everywhere(lambda i: meet(barrier, is_up(i), at_chip(i, core)))
-    for step in sides:
+    opposite = (1,) if chips == 4 else sides
+    for step in opposite:
         meet(barrier, is_up(step), at_chip(step, 1 - core))
     for hop in direct:
         meet(barrier, rep_is_up(*hop), {"rep": rep_of(*hop)})
     pl.semaphore_signal(barrier, inc=1, device_id=partner)
-    ups = number_of([is_up(step) for step in sides])
+    ups = number_of([is_up(step) for step in opposite])
+    downs = number_of([chip > 0]) if chips == 4 else 2 - ups
     rep_ups = number_of([rep_is_up(*hop) for hop in direct])
     with jax.named_scope("barrier"):
-        pl.semaphore_wait(barrier, chip + (2 - ups) + (len(direct) - rep_ups) + 1)
+        pl.semaphore_wait(barrier, chip + downs + (len(direct) - rep_ups) + 1)
     meet(allow.at[0], lower(is_up(-1)), at_chip(-1, core))
     everywhere(lambda i: meet(allow.at[1], lower(is_up(i)), at_chip(i, core)))
     for hop in direct:
         meet(allow.at[2], lower(rep_is_up(*hop)), {"rep": rep_of(*hop)})
-    for step in sides:
-        meet(allow.at[3], lower(is_up(step)), at_chip(step, 1 - core))
+    if chips == 4:
+        meet(allow.at[3], chip > 0, at_chip(-1, 1 - core))
+    else:
+        for step in sides:
+            meet(allow.at[3], lower(is_up(step)), at_chip(step, 1 - core))
 
     def remote(src, dst, send_sem, recv_sem, device):
         return pltpu.make_async_remote_copy(
@@ -305,7 +310,7 @@
         arrive(piece, f_recv.at[h] if slot == FAR else z_recv.at[slot, h])
         if slot != FAR:
             pl.when(passes(slot))(lambda: pass_on(slot, h).start())
-        if mode == ROUTED:
+        if mode == ROUTED and slot != NEAR:
             for number in range(len(diagonal)):
                 routed_copy(slot, number, h).start()
         for t in range(len(direct)):
@@ -396,10 +401,20 @@
             with jax.named_scope(name):
                 if name == "up":
                     up()
-                elif name in ("inward", "outward"):
-                    if extra(role)[name == "outward"]:
+                elif name in ("inward", "outward", "outward0", "outward1"):
+                    if extra(role)[name != "inward"]:
                         for step in sides:
-                            pl.when((way == step) == (name == "inward"))(lambda: send_wide(step))
+                            when = (way == step) == (name == "inward")
+                            if name[-1].isdigit():
+                                when = jnp.logical_and(when, core == int(name[-1]))
+                            pl.when(when)(lambda: send_wide(step))
+                elif name == "corner":
+                    if direct:
+                        pl.semaphore_wait(allow.at[4], len(direct))
+                    if MODES[role][NEAR] == ROUTED:
+                        for h in range(2):
+                            for number in range(len(diagonal)):
+                                routed_copy(NEAR, number, h).start()
                 elif name == "rows":
                     add_rows()
                 elif name[0] == "z":
@@ -451,6 +466,8 @@
     with jax.named_scope("allow"):
         allowed(2, rep_ups)
         allowed(3, ups)
+        for hop in direct:
+            pl.semaphore_signal(allow.at[4], inc=1, device_id={"rep": rep_of(*hop)})
     def body(i, carry):
         for j in range(3):
             pl.when(i == j)(lambda: by_role(j))
@@ -516,7 +533,7 @@
                 pltpu.VMEM((2, count, fields // 2), jnp.bfloat16),
                 pltpu.VMEM((n_vec // 2 + 1, count, fields // 2), jnp.bfloat16),
                 dma((2,)), dma((2, 3)), dma((3,)), dma((3, 2)), dma((3,)), dma((3,)), dma((2,)),
-                dma((1,)), dma((2,)), pltpu.SemaphoreType.REGULAR((4,)),
+                dma((1,)), dma((2,)), pltpu.SemaphoreType.REGULAR((5,)),
             ],
             compiler_params=pltpu.CompilerParams(
                 collective_id=0, has_side_effects=True, vmem_limit_bytes=60_800_000

time: 18.2 us -> 17.6 us (0.967)
  the two profiles are of different devices: /device:TPU:25 before, /device:TPU:0 now
where the time goes in v5:
time: 17.6 us; the launch traced here: 17.3 us
  Pallas kernels  17.3 us (98%)
    pallas_call x1, Pallas kernels, step(): pl.pallas_call(functools.partial(kernel, n_vec, n_a, n_b), out_shape=(plt...  15.4 us
    pallas_call x1, Pallas kernels, step(): pl.pallas_call(functools.partial(closing, n_vec), out_shape=jax.ShapeDtyp...  1.92 us

profile of v5, /device:TPU:0, one launch (start us, length us, event | category | flops | bytes accessed | tf_op | source)
XLA Modules:
  0.0 17.3 jit_solution(10796626016383235513)
XLA Ops:
  0.0 15.4 %shard_map.28 = (bf16[7,8,128,128]{3,2,1,0:T(8,128)(2,1)S(1)}, bf16[7,128,1024]{2,1,0:T(8,128)(2,1)S(1)}, bf16[1024,1024]{1,0:T(8,128)(2,1)S(1)}) custom-call(bf16[128,1024]{1,0:T(8,128)(2,1)} %vec_ref.1, s32[1,8]{1,0:T(1,128)} %index_ref.1), custom_call_target="tpu_custom_call" | custom-call | tf_op jit(solution)/shard_map/pallas_call | solution.py:521
  15.4 1.9 %shard_map.29 = bf16[7,8,128,128]{3,2,1,0:T(8,128)(2,1)} custom-call(bf16[7,8,128,128]{3,2,1,0:T(8,128)(2,1)S(1)} %get-tuple-element.8.held, bf16[7,128,1024]{2,1,0:T(8,128)(2,1)S(1)} %get-tuple-element.9.win, bf16[1024,1024]{1,0:T(8,128)(2,1)S(1)} %get-tuple-element.10.scaled), custom_call_target="tpu_custom_call" | custom-call | tf_op jit(solution)/shard_map/pallas_call | solution.py:542

commit v6 on v5

--- a/solution.py
+++ b/solution.py
@@ -31,8 +31,8 @@
 
 STEPS = (
     (
-        words("z00 up z01 inward", "outward corner z10 z11", "z20 z21 d00 d01", "rows r0"),
-        words("d10 d11 r1 h0"),
+        words("up z00 z01 inward", "outward corner z10 z11", "z20 rows z21"),
+        words("d00 d01 r0 d10", "d11 r1 h0"),
         words("h1"),
         words("d20 d21 r2"),
     ),
@@ -43,14 +43,14 @@
         words("d20 d21 r2"),
     ),
     (
-        words("up inward z00 z10", "z11 z01 corner d00", "rows d01 z20 z21", "r1 d10 d11 r0"),
-        words("h1"),
+        words("up inward z00 z10", "z11 z01 corner d00", "rows d01 z20 z21", "r1 d10 d11"),
+        words("r0 h1"),
         words("h0"),
         words("d20 d21 r2"),
     ),
     (
-        words("up z00 outward0 z01", "inward corner z10 outward1", "z11 z20 z21 d00", "d01 rows r0"),
-        words("d10 d11 r1 h0"),
+        words("up z00 outward0 z01", "inward corner z10 outward1", "z11 z20 rows z21", "d00 d01"),
+        words("r0 d10 d11 r1", "h0"),
         words("h1"),
         words("d20 d21 r2"),
     ),

time: 17.6 us -> 17.5 us (level)
  no operation moved by 1% of the time
where the time goes in v6:
time: 17.5 us; the launch traced here: 17.3 us
  Pallas kernels  17.3 us (99%)
    pallas_call x1, Pallas kernels, step(): pl.pallas_call(functools.partial(kernel, n_vec, n_a, n_b), out_shape=(plt...  15.4 us
    pallas_call x1, Pallas kernels, step(): pl.pallas_call(functools.partial(closing, n_vec), out_shape=jax.ShapeDtyp...  1.92 us

profile of v6, /device:TPU:0, one launch (start us, length us, event | category | flops | bytes accessed | tf_op | source)
XLA Modules:
  0.0 17.3 jit_solution(16126765808202479178)
XLA Ops:
  0.0 15.4 %shard_map.28 = (bf16[7,8,128,128]{3,2,1,0:T(8,128)(2,1)S(1)}, bf16[7,128,1024]{2,1,0:T(8,128)(2,1)S(1)}, bf16[1024,1024]{1,0:T(8,128)(2,1)S(1)}) custom-call(bf16[128,1024]{1,0:T(8,128)(2,1)} %vec_ref.1, s32[1,8]{1,0:T(1,128)} %index_ref.1), custom_call_target="tpu_custom_call" | custom-call | tf_op jit(solution)/shard_map/pallas_call | solution.py:521
  15.4 1.9 %shard_map.29 = bf16[7,8,128,128]{3,2,1,0:T(8,128)(2,1)} custom-call(bf16[7,8,128,128]{3,2,1,0:T(8,128)(2,1)S(1)} %get-tuple-element.8.held, bf16[7,128,1024]{2,1,0:T(8,128)(2,1)S(1)} %get-tuple-element.9.win, bf16[1024,1024]{1,0:T(8,128)(2,1)S(1)} %get-tuple-element.10.scaled), custom_call_target="tpu_custom_call" | custom-call | tf_op jit(solution)/shard_map/pallas_call | solution.py:542

commit v7 on v6

--- a/solution.py
+++ b/solution.py
@@ -221,10 +221,10 @@
     for hop in direct:
         meet(allow.at[2], lower(rep_is_up(*hop)), {"rep": rep_of(*hop)})
     if chips == 4:
-        meet(allow.at[3], chip > 0, at_chip(-1, 1 - core))
+        meet(allow.at[2], chip > 0, at_chip(-1, 1 - core))
     else:
         for step in sides:
-            meet(allow.at[3], lower(is_up(step)), at_chip(step, 1 - core))
+            meet(allow.at[2], lower(is_up(step)), at_chip(step, 1 - core))
 
     def remote(src, dst, send_sem, recv_sem, device):
         return pltpu.make_async_remote_copy(
@@ -261,7 +261,7 @@
             rows = pl.ds(pl.multiple_of(rep_of(*diagonal[which - 2]) * part, part), part)
         return remote(
             vec_ref.at[rows], win.at[AT[NEAR] + (AT[OUTER] - AT[NEAR]) * slot, rows],
-            out_sem.at[0], z_recv.at[slot, jnp.minimum(which, 2)], at_chip(step, core),
+            out_sem.at[0], z_recv.at[slot, which] if which < 2 else r_recv.at[slot], at_chip(step, core),
         )
 
     def passes(slot):
@@ -328,16 +328,12 @@
 
     def third(slot, mode, role):
         if diagonal:
-            if mode != WIDE:
-                sem = r_recv.at[slot]
-            else:
-                sem = f_recv.at[2] if slot == FAR else z_recv.at[slot, 2]
-            arrive(len(diagonal) * part, sem)
+            arrive(len(diagonal) * part, r_recv.at[slot])
         if slot == NEAR and widens(role):
             for spot in diagonal:
                 rows = pl.ds(pl.multiple_of(rep_of(*spot) * part, part), part)
                 remote(
-                    win.at[AT[NEAR], rows], win.at[AT[FAR], rows], out_sem.at[0], f_recv.at[2],
+                    win.at[AT[NEAR], rows], win.at[AT[FAR], rows], out_sem.at[0], r_recv.at[FAR],
                     at_chip(-way, 1 - core),
                 ).start()
         for spot in diagonal:
@@ -410,7 +406,7 @@
                             pl.when(when)(lambda: send_wide(step))
                 elif name == "corner":
                     if direct:
-                        pl.semaphore_wait(allow.at[4], len(direct))
+                        pl.semaphore_wait(allow.at[3], len(direct))
                     if MODES[role][NEAR] == ROUTED:
                         for h in range(2):
                             for number in range(len(diagonal)):
@@ -464,10 +460,9 @@
         send_z(1, range(2))
 
     with jax.named_scope("allow"):
-        allowed(2, rep_ups)
-        allowed(3, ups)
+        allowed(2, rep_ups + ups)
         for hop in direct:
-            pl.semaphore_signal(allow.at[4], inc=1, device_id={"rep": rep_of(*hop)})
+            pl.semaphore_signal(allow.at[3], inc=1, device_id={"rep": rep_of(*hop)})
     def body(i, carry):
         for j in range(3):
             pl.when(i == j)(lambda: by_role(j))
@@ -532,8 +527,8 @@
                 pltpu.VMEM((2, count, fields // 2), jnp.bfloat16),
                 pltpu.VMEM((2, count, fields // 2), jnp.bfloat16),
                 pltpu.VMEM((n_vec // 2 + 1, count, fields // 2), jnp.bfloat16),
-                dma((2,)), dma((2, 3)), dma((3,)), dma((3, 2)), dma((3,)), dma((3,)), dma((2,)),
-                dma((1,)), dma((2,)), pltpu.SemaphoreType.REGULAR((5,)),
+                dma((2,)), dma((2, 2)), dma((2,)), dma((3, 2)), dma((3,)), dma((3,)), dma((2,)),
+                dma((1,)), dma((2,)), pltpu.SemaphoreType.REGULAR((4,)),
             ],
             compiler_params=pltpu.CompilerParams(
                 collective_id=0, has_side_effects=True, vmem_limit_bytes=60_800_000

time: 17.5 us -> 17.5 us (level)
  no operation moved by 1% of the time
where the time goes in v7:
time: 17.5 us; the launch traced here: 17.3 us
  Pallas kernels  17.3 us (99%)
    pallas_call x1, Pallas kernels, step(): pl.pallas_call(functools.partial(kernel, n_vec, n_a, n_b), out_shape=(plt...  15.4 us
    pallas_call x1, Pallas kernels, step(): pl.pallas_call(functools.partial(closing, n_vec), out_shape=jax.ShapeDtyp...  1.92 us

profile of v7, /device:TPU:0, one launch (start us, length us, event | category | flops | bytes accessed | tf_op | source)
XLA Modules:
  0.0 17.3 jit_solution(17076732546197867019)
XLA Ops:
  0.0 15.4 %shard_map.28 = (bf16[7,8,128,128]{3,2,1,0:T(8,128)(2,1)S(1)}, bf16[7,128,1024]{2,1,0:T(8,128)(2,1)S(1)}, bf16[1024,1024]{1,0:T(8,128)(2,1)S(1)}) custom-call(bf16[128,1024]{1,0:T(8,128)(2,1)} %vec_ref.1, s32[1,8]{1,0:T(1,128)} %index_ref.1), custom_call_target="tpu_custom_call" | custom-call | tf_op jit(solution)/shard_map/pallas_call | solution.py:516
  15.4 1.9 %shard_map.29 = bf16[7,8,128,128]{3,2,1,0:T(8,128)(2,1)} custom-call(bf16[7,8,128,128]{3,2,1,0:T(8,128)(2,1)S(1)} %get-tuple-element.8.held, bf16[7,128,1024]{2,1,0:T(8,128)(2,1)S(1)} %get-tuple-element.9.win, bf16[1024,1024]{1,0:T(8,128)(2,1)S(1)} %get-tuple-element.10.scaled), custom_call_target="tpu_custom_call" | custom-call | tf_op jit(solution)/shard_map/pallas_call | solution.py:537

commit v8 on v7

--- a/solution.py
+++ b/solution.py
@@ -31,8 +31,8 @@
 
 STEPS = (
     (
-        words("up z00 z01 inward", "outward corner z10 z11", "z20 rows z21"),
-        words("d00 d01 r0 d10", "d11 r1 h0"),
+        words("up z00 z01 inward", "outward corner z10 z11", "z20 rows z21 d00", "d01"),
+        words("r0 d10 d11 r1", "h0"),
         words("h1"),
         words("d20 d21 r2"),
     ),

time: 17.5 us -> 17.5 us (level)
  no operation moved by 1% of the time
where the time goes in v8:
time: 17.5 us; the launch traced here: 17.3 us
  Pallas kernels  17.3 us (99%)
    pallas_call x1, Pallas kernels, step(): pl.pallas_call(functools.partial(kernel, n_vec, n_a, n_b), out_shape=(plt...  15.4 us
    pallas_call x1, Pallas kernels, step(): pl.pallas_call(functools.partial(closing, n_vec), out_shape=jax.ShapeDtyp...  1.92 us

profile of v8, /device:TPU:0, one launch (start us, length us, event | category | flops | bytes accessed | tf_op | source)
XLA Modules:
  0.0 17.3 jit_solution(3436681708460222845)
XLA Ops:
  0.0 15.4 %shard_map.28 = (bf16[7,8,128,128]{3,2,1,0:T(8,128)(2,1)S(1)}, bf16[7,128,1024]{2,1,0:T(8,128)(2,1)S(1)}, bf16[1024,1024]{1,0:T(8,128)(2,1)S(1)}) custom-call(bf16[128,1024]{1,0:T(8,128)(2,1)} %vec_ref.1, s32[1,8]{1,0:T(1,128)} %index_ref.1), custom_call_target="tpu_custom_call" | custom-call | tf_op jit(solution)/shard_map/pallas_call | solution.py:516
  15.4 1.9 %shard_map.29 = bf16[7,8,128,128]{3,2,1,0:T(8,128)(2,1)} custom-call(bf16[7,8,128,128]{3,2,1,0:T(8,128)(2,1)S(1)} %get-tuple-element.8.held, bf16[7,128,1024]{2,1,0:T(8,128)(2,1)S(1)} %get-tuple-element.9.win, bf16[1024,1024]{1,0:T(8,128)(2,1)S(1)} %get-tuple-element.10.scaled), custom_call_target="tpu_custom_call" | custom-call | tf_op jit(solution)/shard_map/pallas_call | solution.py:537

commit v9 on v8

--- a/solution.py
+++ b/solution.py
@@ -31,7 +31,7 @@
 
 STEPS = (
     (
-        words("up z00 z01 inward", "outward corner z10 z11", "z20 rows z21 d00", "d01"),
+        words("up z00 z01 inward", "outward corner z10 z11", "rows z20 z21 d00", "d01"),
         words("r0 d10 d11 r1", "h0"),
         words("h1"),
         words("d20 d21 r2"),

time: 17.5 us -> 17.5 us (level)
  no operation moved by 1% of the time
where the time goes in v9:
time: 17.5 us; the launch traced here: 17.3 us
  Pallas kernels  17.3 us (99%)
    pallas_call x1, Pallas kernels, step(): pl.pallas_call(functools.partial(kernel, n_vec, n_a, n_b), out_shape=(plt...  15.4 us
    pallas_call x1, Pallas kernels, step(): pl.pallas_call(functools.partial(closing, n_vec), out_shape=jax.ShapeDtyp...  1.92 us

profile of v9, /device:TPU:0, one launch (start us, length us, event | category | flops | bytes accessed | tf_op | source)
XLA Modules:
  0.0 17.3 jit_solution(12580866802494373143)
XLA Ops:
  0.0 15.4 %shard_map.28 = (bf16[7,8,128,128]{3,2,1,0:T(8,128)(2,1)S(1)}, bf16[7,128,1024]{2,1,0:T(8,128)(2,1)S(1)}, bf16[1024,1024]{1,0:T(8,128)(2,1)S(1)}) custom-call(bf16[128,1024]{1,0:T(8,128)(2,1)} %vec_ref.1, s32[1,8]{1,0:T(1,128)} %index_ref.1), custom_call_target="tpu_custom_call" | custom-call | tf_op jit(solution)/shard_map/pallas_call | solution.py:516
  15.4 1.9 %shard_map.29 = bf16[7,8,128,128]{3,2,1,0:T(8,128)(2,1)} custom-call(bf16[7,8,128,128]{3,2,1,0:T(8,128)(2,1)S(1)} %get-tuple-element.8.held, bf16[7,128,1024]{2,1,0:T(8,128)(2,1)S(1)} %get-tuple-element.9.win, bf16[1024,1024]{1,0:T(8,128)(2,1)S(1)} %get-tuple-element.10.scaled), custom_call_target="tpu_custom_call" | custom-call | tf_op jit(solution)/shard_map/pallas_call | solution.py:537
